TPU v7x, 256 devices: a whole 4x4x8 slice. The times are simulated.
256 devices in a mesh: section: 8 (over z_lo, core), dp: 32 (over z_hi, x, y).
Axes of the slice: x: 4, y: 4, z: 8 (z_hi: 2, z_lo: 4; z = z_hi * 4 + z_lo), core: 2. Of those that a mesh axis runs over, the one named last changes fastest.
Arguments:
- token_grad: bfloat16 [65536, 4608], P(('section', 'dp')), may hold values from -6 to 6
- owner: int32 [65536, 1], P(('section', 'dp')), may hold values from 0 to 255; in each aligned block of 256 rows (0 to 255, 256 to 511, ...) at most 2 rows name the same one
- local_row: int32 [65536], P(('section', 'dp')), may hold values from 0 to 999
Outputs:
- vocab_grad: bfloat16 [256000, 4608], P(('section', 'dp'))
Inputs may be any that keep to these rules, and one draw needn't show every extreme that they name: `owner`: among the rows of one device, no shard is named more than 2 times, a bound that some block reaches.
All inputs are finite; a program needn't handle non-finite values.
Results may differ from a plain program's by a relative error of at most 0.001.
Values may be sent and summed in bfloat16 or wider, within the bound.
A program may use at most 64 MiB of HBM per device.

v0:
```python
import jax
import jax.numpy as jnp
from jax import lax
from jax.sharding import PartitionSpec as P

VROWS_DEV = 1000


def per_device(token_grad, owner, local_row):
    section_count = lax.axis_size("section")
    data_count = lax.axis_size("dp")
    owner_count = section_count * data_count
    width = token_grad.shape[1]
    capacity = max(2, 2 * token_grad.shape[0] // owner_count)
    slot_total = owner_count * capacity
    destination = owner[:, 0]
    matches = (destination[:, None] == jnp.arange(owner_count, dtype=jnp.int32)[None, :]).astype(
        jnp.int32
    )
    slot_rank = jnp.sum(jnp.cumsum(matches, axis=0) * matches, axis=1) - 1
    slot_index = destination * capacity + slot_rank
    send_rows = jnp.zeros((slot_total, width), jnp.bfloat16).at[slot_index].set(token_grad)
    send_ids = jnp.full((slot_total,), -1, jnp.int32).at[slot_index].set(local_row)
    send_rows = send_rows.reshape(section_count, data_count, capacity, width)
    send_ids = send_ids.reshape(section_count, data_count, capacity)
    got_rows, got_ids = (
        lax.all_to_all(
            lax.all_to_all(send_rows, "section", split_axis=0, concat_axis=0, tiled=True),
            "dp",
            split_axis=1,
            concat_axis=1,
            tiled=True,
        ),
        lax.all_to_all(
            lax.all_to_all(send_ids, "section", split_axis=0, concat_axis=0, tiled=True),
            "dp",
            split_axis=1,
            concat_axis=1,
            tiled=True,
        ),
    )
    got_rows = got_rows.reshape(slot_total, width)
    got_ids = got_ids.reshape(slot_total)
    selector = (jnp.arange(VROWS_DEV, dtype=jnp.int32)[:, None] == got_ids[None, :]).astype(
        jnp.bfloat16
    )
    summed = jnp.dot(selector, got_rows, preferred_element_type=jnp.float32)
    return summed.astype(jnp.bfloat16)


def solution(mesh):
    return jax.shard_map(
        per_device,
        mesh=mesh,
        in_specs=(P(("section", "dp"), None), P(("section", "dp"), None), P(("section", "dp"))),
        out_specs=P(("section", "dp"), None),
        check_vma=False,
    )
```

profile of v0, /device:TPU:1, one launch (start us, length us, event | category | flops | bytes accessed | tf_op | source)
XLA Modules:
  0.0 298.4 jit_solution(8345672531331131793)
XLA Ops:
  0.0 0.8 copy.20
  0.8 0.2 fusion.3
  1.1 0.9 fusion.4
  2.0 0.7 compare_select_fusion
  2.7 1.6 scatter_custom_fusion
  4.2 0.1 reshape.36
  4.4 0.7 copy.22
  5.1 7.4 %all-to-all-start = ((s32[8,32,2]{1,2,0:T(2,128)}), s32[8,32,2]{1,2,0:T(2,128)S(1)}, u32[]{:S(2)}, u32[]{:S(2)}) async-start(s32[8,32,2]{1,2,0:T(2,128)} %copy.22), calls=%async_computation | async-start | bytes 16384 | tf_op jit(solution)/shard_map/all_to_all | solution.py:35
  12.5 7.8 %scatter_custom_fusion.1 = bf16[512,4608]{1,0:T(8,128)(2,1)} fusion(s32[256]{0:T(256)S(1)} %bitcast.25, bf16[256,4608]{1,0:T(8,128)(2,1)} %param.3, bf16[]{:T(256)} %constant.16.clone.1), kind=kCustom, calls=%fused_computation.3 | custom fusion | bytes 4719104 | tf_op jit(solution)/shard_map/scatter | solution.py:22
  20.3 7.5 %reshape.37 = bf16[8,32,2,4608]{3,2,1,0:T(2,128)(2,1)} reshape(bf16[512,4608]{1,0:T(8,128)(2,1)} %scatter_custom_fusion.1) | data formatting | bytes 9437184 | tf_op jit(solution)/shard_map/reshape | solution.py:24
  27.8 0.0 all-to-all-done
  27.8 5.1 %all-to-all-start.2 = ((bf16[8,32,2,4608]{3,2,1,0:T(2,128)(2,1)}), bf16[8,32,2,4608]{3,2,1,0:T(2,128)(2,1)}, u32[]{:S(2)}, u32[]{:S(2)}) async-start(bf16[8,32,2,4608]{3,2,1,0:T(2,128)(2,1)} %reshape.37), calls=%async_computation.2 | async-start | bytes 9437184 | tf_op jit(solution)/shard_map/all_to_all | solution.py:28
  32.9 0.7 copy.23
  33.6 103.7 %all-to-all-done.2 = bf16[8,32,2,4608]{3,2,1,0:T(2,128)(2,1)} async-done(((bf16[8,32,2,4608]{3,2,1,0:T(2,128)(2,1)}), bf16[8,32,2,4608]{3,2,1,0:T(2,128)(2,1)}, u32[]{:S(2)}, u32[]{:S(2)}) %all-to-all-start.2) | async-done | bytes 4718624 | tf_op jit(solution)/shard_map/all_to_all | solution.py:28
  137.3 11.0 %all-to-all-start.1 = ((s32[8,32,2]{0,2,1:T(2,128)}), s32[8,32,2]{0,2,1:T(2,128)S(1)}, u32[]{:S(2)}, u32[]{:S(2)}) async-start(s32[8,32,2]{0,2,1:T(2,128)} %copy.23), calls=%async_computation.1 | async-start | bytes 65536 | tf_op jit(solution)/shard_map/all_to_all | solution.py:34
  148.3 9.4 %copy.25 = bf16[8,32,2,4608]{3,2,0,1:T(2,128)(2,1)} copy(bf16[8,32,2,4608]{3,2,1,0:T(2,128)(2,1)} %all-to-all-done.2) | data formatting | bytes 9437184 | tf_op jit(solution)/shard_map/all_to_all | solution.py:28
  157.7 1.6 all-to-all-done.1
  159.3 10.1 %all-to-all-start.3 = ((bf16[8,32,2,4608]{3,2,0,1:T(2,128)(2,1)}), bf16[8,32,2,4608]{3,2,0,1:T(2,128)(2,1)}, u32[]{:S(2)}, u32[]{:S(2)}) async-start(bf16[8,32,2,4608]{3,2,0,1:T(2,128)(2,1)} %copy.25), calls=%async_computation.3 | async-start | bytes 9437184 | tf_op jit(solution)/shard_map/all_to_all | solution.py:27
  169.5 0.3 copy.24
  169.8 0.1 eq.49
  169.9 103.5 %all-to-all-done.3 = bf16[8,32,2,4608]{3,2,0,1:T(2,128)(2,1)} async-done(((bf16[8,32,2,4608]{3,2,0,1:T(2,128)(2,1)}), bf16[8,32,2,4608]{3,2,0,1:T(2,128)(2,1)}, u32[]{:S(2)}, u32[]{:S(2)}) %all-to-all-start.3) | async-done | bytes 4718624 | tf_op jit(solution)/shard_map/all_to_all | solution.py:27
  273.4 7.8 %copy.26 = bf16[8,32,2,4608]{3,2,1,0:T(2,128)(2,1)} copy(bf16[8,32,2,4608]{3,2,0,1:T(2,128)(2,1)} %all-to-all-done.3) | data formatting | bytes 9437184 | tf_op jit(solution)/shard_map/all_to_all | solution.py:27
  281.2 7.5 %reshape.38 = bf16[512,4608]{1,0:T(8,128)(2,1)} reshape(bf16[8,32,2,4608]{3,2,1,0:T(2,128)(2,1)} %copy.26) | data formatting | bytes 9437184 | tf_op jit(solution)/shard_map/reshape | solution.py:42
  288.7 9.6 %convolution_convert_fusion = bf16[1000,4608]{1,0:T(8,128)(2,1)} fusion(bf16[512,4608]{1,0:T(8,128)(2,1)} %reshape.38, s32[512]{0:T(512)S(1)} %eq.49), kind=kOutput, calls=%fused_computation.2 | convolution fusion | flops 4723712000 | bytes 13936640 | tf_op jit(solution)/shard_map/dot_general | solution.py:47
  (7 shorter events, 0.1 us)
Async XLA Ops:
  5.1 22.7 %all-to-all-start = ((s32[8,32,2]{1,2,0:T(2,128)}), s32[8,32,2]{1,2,0:T(2,128)S(1)}, u32[]{:S(2)}, u32[]{:S(2)}) async-start(s32[8,32,2]{1,2,0:T(2,128)} %copy.22), calls=%async_computation | async-start | bytes 16384 | tf_op jit(solution)/shard_map/all_to_all | solution.py:35
  27.8 109.4 %all-to-all-start.2 = ((bf16[8,32,2,4608]{3,2,1,0:T(2,128)(2,1)}), bf16[8,32,2,4608]{3,2,1,0:T(2,128)(2,1)}, u32[]{:S(2)}, u32[]{:S(2)}) async-start(bf16[8,32,2,4608]{3,2,1,0:T(2,128)(2,1)} %reshape.37), calls=%async_computation.2 | async-start | bytes 9437184 | tf_op jit(solution)/shard_map/all_to_all | solution.py:28
  137.3 22.1 %all-to-all-start.1 = ((s32[8,32,2]{0,2,1:T(2,128)}), s32[8,32,2]{0,2,1:T(2,128)S(1)}, u32[]{:S(2)}, u32[]{:S(2)}) async-start(s32[8,32,2]{0,2,1:T(2,128)} %copy.23), calls=%async_computation.1 | async-start | bytes 65536 | tf_op jit(solution)/shard_map/all_to_all | solution.py:34
  159.3 114.1 %all-to-all-start.3 = ((bf16[8,32,2,4608]{3,2,0,1:T(2,128)(2,1)}), bf16[8,32,2,4608]{3,2,0,1:T(2,128)(2,1)}, u32[]{:S(2)}, u32[]{:S(2)}) async-start(bf16[8,32,2,4608]{3,2,0,1:T(2,128)(2,1)} %copy.25), calls=%async_computation.3 | async-start | bytes 9437184 | tf_op jit(solution)/shard_map/all_to_all | solution.py:27
where the time goes:
time: 303 us; the launch traced here: 298 us
  waiting for transfers between devices  209 us (69%)
  local copies, waits for them, and re-layouts  44.4 us (15%)
  starting transfers between devices  33.6 us (11%)
  matrix products  9.62 us (3%)
    all_to_all x1, waiting for transfers between devices, per_device(): lax.all_to_all(send_rows, 'section', split_axis=0, concat_axis=0, tiled=T...  104 us
    all_to_all x1, waiting for transfers between devices, per_device(): lax.all_to_all(lax.all_to_all(send_rows, 'section', split_axis=0, concat_...  104 us
    all_to_all x1, starting transfers between devices, per_device(): lax.all_to_all(lax.all_to_all(send_ids, 'section', split_axis=0, concat_a...  11 us
    all_to_all x1, starting transfers between devices, per_device(): lax.all_to_all(lax.all_to_all(send_rows, 'section', split_axis=0, concat_...  10.1 us
    dot_general x1, matrix products, per_device(): summed = jnp.dot(selector, got_rows, preferred_element_type=jnp.float32)  9.62 us
    all_to_all x1, local copies, waits for them, and re-layouts, per_device(): lax.all_to_all(send_rows, 'section', split_axis=0, concat_axis=0, tiled=T...  9.43 us
    scatter x1, local copies, waits for them, and re-layouts, per_device(): jnp.zeros((slot_total, width), jnp.bfloat16).at[slot_index].set(token_grad)  7.79 us
    all_to_all x1, local copies, waits for them, and re-layouts, per_device(): lax.all_to_all(lax.all_to_all(send_rows, 'section', split_axis=0, concat_...  7.76 us
  transfers between devices with their start and end apart: 4, of which 3 were waited for; matrix products, arithmetic and copies ran while one was open for 9% of the time, Pallas kernels for 0%

commit v1 on v0

v1 whole, which is shorter than its diff:
```python
import functools

import jax
import jax.numpy as jnp
from jax import lax
from jax.experimental import pallas as pl
from jax.experimental.pallas import tpu as pltpu
from jax.sharding import PartitionSpec as P

VROWS_DEV = 1000
Z_HI, Z_LO, CORES = 2, 4, 2
COLUMNS = 512
LANES = 128
MESH = pl.DeviceIdType.MESH
F32, BF16, I32 = jnp.float32, jnp.bfloat16, jnp.int32


def log2(n):
    return n.bit_length() - 1


def kernel(z_n, z_lo_n, core_n, xy_n, cap, x_ref, owner_ref, row_ref, out_ref,
           pack, send, zgot, spread, got, sel2, selector, smeta, zmeta, pmeta, gmeta, stage,
           zs_sem, zr_sem, ps_sem, pr_sem, zm_sem, pm_sem, ms_sem, o_sem):
    chunks, wide = send.shape[0], send.shape[2]
    tokens = x_ref.shape[0]
    p_n = xy_n * core_n
    slab = 2 * z_n
    dp_n = (z_n // z_lo_n) * xy_n
    s, d = lax.axis_index("section"), lax.axis_index("dp")
    my_lo, my_core = s // core_n, s % core_n
    my_hi, my_xy = d // xy_n, d % xy_n
    my_z = my_hi * z_lo_n + my_lo
    my_p = my_xy * core_n + my_core

    def z_peer(k):
        z = (my_z + k) % z_n
        return (z % z_lo_n) * core_n + my_core, (z // z_lo_n) * xy_n + my_xy

    def p_peer(k):
        p = (my_p + k) % p_n
        return my_lo * core_n + p % core_n, my_hi * xy_n + p // core_n

    barrier = pltpu.get_barrier_semaphore()

    def greet_z(k, carry):
        pl.semaphore_signal(barrier, inc=1, device_id=z_peer(k), device_id_type=MESH)
        return carry

    def greet_p(k, carry):
        pl.semaphore_signal(barrier, inc=1, device_id=p_peer(k), device_id_type=MESH)
        return carry

    lax.fori_loop(1, z_n, greet_z, 0)
    lax.fori_loop(1, p_n, greet_p, 0)

    ii = lax.broadcasted_iota(I32, (tokens, tokens), 0)
    jj = lax.broadcasted_iota(I32, (tokens, tokens), 1)

    def to_row(col):
        return jnp.sum(jnp.where(ii == jj, col, 0.0), axis=0, keepdims=True)

    def to_col(row):
        return jnp.sum(jnp.where(ii == jj, row, 0.0), axis=1, keepdims=True)

    own = owner_ref[...]
    own_s, own_d = own >> log2(dp_n), own & (dp_n - 1)
    own_z = (own_d >> log2(xy_n)) * z_lo_n + (own_s >> log2(core_n))
    own_p = (own_d & (xy_n - 1)) * core_n + (own_s & (core_n - 1))
    far = (own_z - my_z + z_n) & (z_n - 1)
    near = (own_p - my_p + p_n) & (p_n - 1)
    own_f, far_f = own.astype(F32), far.astype(F32)
    own_row, far_row = to_row(own_f), to_row(far_f)
    twin = jnp.sum(jnp.where((own_f == own_row) & (jj < ii), 1.0, 0.0), axis=1, keepdims=True)
    place = jnp.sum(jnp.where((far_f == far_row) & (ii < jj), 1.0, 0.0), axis=0, keepdims=True)
    spot = far_row * cap + place
    slots = lax.broadcasted_iota(I32, (z_n * cap, tokens), 0).astype(F32)
    pack[...] = jnp.where(slots == spot, 1.0, 0.0).astype(BF16)
    row = to_col(row_ref[...].astype(F32)).astype(I32)
    lane = lax.broadcasted_iota(I32, (tokens, LANES), 1)
    meta = jnp.where(lane == 0, near.astype(F32), 0.0)
    meta = jnp.where(lane == 1, 2.0 * far_f + twin, meta)
    meta = jnp.where(lane == 2, (row >> 5).astype(F32), meta)
    meta = jnp.where(lane == 3, (row & 31).astype(F32), meta)
    meta = jnp.where(lane == 4, 1.0, meta).astype(BF16)
    packed = jnp.dot(pack[...], meta, preferred_element_type=F32).astype(BF16)
    zmeta[0:cap, :] = packed[0:cap]
    smeta[...] = packed[cap:]

    def z_copy(k, src, dst, ssem, rsem):
        return pltpu.make_async_remote_copy(src, dst, ssem, rsem, device_id=z_peer(k), device_id_type=MESH)

    def p_copy(k, src, dst, ssem, rsem):
        return pltpu.make_async_remote_copy(src, dst, ssem, rsem, device_id=p_peer(k), device_id_type=MESH)

    def pack_chunk(j):
        cols = pl.ds(pl.multiple_of(j * wide, wide), wide)
        part = jnp.dot(pack[...], x_ref[:, cols], preferred_element_type=F32).astype(BF16)
        zgot[j, 0:cap, :] = part[0:cap]
        send[j] = part[cap:]

    order = sorted(range(1, z_n), key=lambda k: -min(k, z_n - k))

    def send_chunk(j):
        for k in order:
            z_copy(k, send.at[j, pl.ds((k - 1) * cap, cap)], zgot.at[j, pl.ds(k * cap, cap)],
                   zs_sem, zr_sem.at[j]).start()

    pack_chunk(0)
    pl.semaphore_wait(barrier, z_n - 1 + p_n - 1)
    for k in order:
        z_copy(k, smeta.at[pl.ds((k - 1) * cap, cap)], zmeta.at[pl.ds(k * cap, cap)], ms_sem, zm_sem).start()
    send_chunk(0)

    def pack_and_send(j, carry):
        pack_chunk(j)
        send_chunk(j)
        return carry

    lax.fori_loop(1, chunks, pack_and_send, 0)

    lane8 = lax.broadcasted_iota(I32, (8, LANES), 1)

    def across(weights, columns):
        w = jnp.zeros((8, LANES), F32)
        for at, value in weights:
            w = jnp.where(lane8 == at, value, w)
        rows = lax.dot_general(w.astype(BF16), columns, (((1,), (1,)), ((), ())), preferred_element_type=F32)
        return rows[0:1] - 1.0

    pltpu.make_async_copy(zmeta.at[pl.ds(cap, (z_n - 1) * cap)], zmeta.at[pl.ds(cap, (z_n - 1) * cap)], zm_sem).wait()
    spot2 = across([(0, float(slab)), (1, 1.0), (4, 1.0)], zmeta[...])
    slots2 = lax.broadcasted_iota(I32, (p_n * slab, z_n * cap), 0).astype(F32)
    sel2[...] = jnp.where(slots2 == spot2, 1.0, 0.0).astype(BF16)
    spread_meta = jnp.dot(sel2[...], zmeta[...], preferred_element_type=F32).astype(BF16)
    gmeta[0:slab, :] = spread_meta[0:slab]
    pmeta[...] = spread_meta[slab:]

    def send_meta(k, carry):
        p_copy(k, pmeta.at[pl.ds((k - 1) * slab, slab)], gmeta.at[pl.ds(k * slab, slab)], ms_sem, pm_sem).start()
        return carry

    rest = (p_n - 1) * slab

    def relay_chunk(j):
        arrived = zgot.at[j, pl.ds(cap, (z_n - 1) * cap)]
        pltpu.make_async_copy(arrived, arrived, zr_sem.at[j]).wait()
        part = jnp.dot(sel2[...], zgot[j], preferred_element_type=F32).astype(BF16)
        got[j, 0:slab, :] = part[0:slab]
        spread[j] = part[slab:]

        def out_to(k, carry):
            p_copy(k, spread.at[j, pl.ds((k - 1) * slab, slab)], got.at[j, pl.ds(k * slab, slab)],
                   ps_sem, pr_sem.at[j]).start()
            return carry

        lax.fori_loop(1, p_n, out_to, 0)

    def out_copy(j):
        return pltpu.make_async_copy(
            stage.at[j], out_ref.at[:, pl.ds(pl.multiple_of(j * wide, wide), wide)], o_sem.at[j])

    def finish_chunk(j):
        arrived = got.at[j, pl.ds(slab, rest)]
        pltpu.make_async_copy(arrived, arrived, pr_sem.at[j]).wait()
        stage[j] = jnp.dot(selector[...], got[j], preferred_element_type=F32).astype(BF16)
        out_copy(j).start()

    lax.fori_loop(1, p_n, send_meta, 0)
    relay_chunk(0)

    arrived = gmeta.at[pl.ds(slab, rest)]
    pltpu.make_async_copy(arrived, arrived, pm_sem).wait()
    mine = across([(2, 32.0), (3, 1.0), (4, 1.0)], gmeta[...])
    vocab = lax.broadcasted_iota(I32, selector.shape, 0).astype(F32)
    selector[...] = jnp.where(vocab == mine, 1.0, 0.0).astype(BF16)

    def step(j, carry):
        relay_chunk(j)
        finish_chunk(j - 1)
        return carry

    lax.fori_loop(1, chunks, step, 0)
    finish_chunk(chunks - 1)

    pltpu.make_async_copy(send, send, zs_sem).wait()
    pltpu.make_async_copy(spread, spread, ps_sem).wait()
    pltpu.make_async_copy(smeta, smeta, ms_sem).wait()
    pltpu.make_async_copy(pmeta, pmeta, ms_sem).wait()

    def drain(j, carry):
        out_copy(j).wait()
        return carry

    lax.fori_loop(0, chunks, drain, 0)


def build(mesh, z_hi, z_lo, cores, vrows, wide):
    section_n, dp_n = mesh.shape["section"], mesh.shape["dp"]
    xy_n = dp_n // z_hi
    z_n, p_n = z_hi * z_lo, xy_n * cores

    def per_device(token_grad, owner, local_row):
        tokens, width = token_grad.shape
        cap = 2 * p_n
        slab = 2 * z_n
        chunks = width // wide
        dma = pltpu.SemaphoreType.DMA
        return pl.pallas_call(
            functools.partial(kernel, z_n, z_lo, cores, xy_n, cap),
            out_shape=jax.ShapeDtypeStruct((vrows, width), BF16),
            in_specs=[pl.BlockSpec(memory_space=pltpu.VMEM)] * 3,
            out_specs=pl.BlockSpec(memory_space=pl.ANY),
            scratch_shapes=[
                pltpu.VMEM((z_n * cap, tokens), BF16),
                pltpu.VMEM((chunks, (z_n - 1) * cap, wide), BF16),
                pltpu.VMEM((chunks, z_n * cap, wide), BF16),
                pltpu.VMEM((chunks, (p_n - 1) * slab, wide), BF16),
                pltpu.VMEM((chunks, p_n * slab, wide), BF16),
                pltpu.VMEM((p_n * slab, z_n * cap), BF16),
                pltpu.VMEM((vrows, p_n * slab), BF16),
                pltpu.VMEM(((z_n - 1) * cap, LANES), BF16),
                pltpu.VMEM((z_n * cap, LANES), BF16),
                pltpu.VMEM(((p_n - 1) * slab, LANES), BF16),
                pltpu.VMEM((p_n * slab, LANES), BF16),
                pltpu.VMEM((chunks, vrows, wide), BF16),
                dma, dma((chunks,)), dma, dma((chunks,)), dma, dma, dma, dma((chunks,)),
            ],
            compiler_params=pltpu.CompilerParams(collective_id=0, has_side_effects=True),
        )(token_grad, owner, local_row.reshape(1, tokens))

    return jax.shard_map(
        per_device,
        mesh=mesh,
        in_specs=(P(("section", "dp"), None), P(("section", "dp"), None), P(("section", "dp"))),
        out_specs=P(("section", "dp"), None),
        check_vma=False,
    )


def solution(mesh):
    return build(mesh, Z_HI, Z_LO, CORES, VROWS_DEV, COLUMNS)
```

time: 303 us -> 139 us (0.46); the launches traced: 298 us -> 139 us
  waiting for transfers between devices: 209 us -> 0 us
  Pallas kernels: 0 us -> 129 us
  local copies, waits for them, and re-layouts: 44.4 us -> 9.35 us
  starting transfers between devices: 33.6 us -> 0 us
  matrix products: 9.62 us -> 0 us
    all_to_all x4 -> x0, waiting for transfers between devices: 209 us -> none  [the longest x1 104 us: per_device(): lax.all_to_all(send_rows, 'section', split_axis=0, concat_axis=0, tiled=T...]
    pallas_call x0 -> x1, Pallas kernels: none -> 129 us  [per_device(): pl.pallas_call(functools.partial(kernel, z_n, z_lo, cores, xy_n, cap), ou...]
    all_to_all x4 -> x0, starting transfers between devices: 33.6 us -> none  [the longest x1 11 us: per_device(): lax.all_to_all(lax.all_to_all(send_ids, 'section', split_axis=0, concat_a...]
    all_to_all x4 -> x0, local copies, waits for them, and re-layouts: 18.1 us -> none  [the longest x1 9.43 us: per_device(): lax.all_to_all(send_rows, 'section', split_axis=0, concat_axis=0, tiled=T...]
    reshape x4 -> x0, local copies, waits for them, and re-layouts: 15.9 us -> none  [the longest x1 7.54 us: per_device(): send_rows = send_rows.reshape(section_count, data_count, capacity, width)]
    dot_general x1 -> x0, matrix products: 9.62 us -> none  [per_device(): summed = jnp.dot(selector, got_rows, preferred_element_type=jnp.float32)]
    unnamed x1 -> x2, local copies, waits for them, and re-layouts: 0.01 us -> 9.35 us
    scatter x2 -> x0, local copies, waits for them, and re-layouts: 9.34 us -> none  [the longest x1 7.79 us: per_device(): jnp.zeros((slot_total, width), jnp.bfloat16).at[slot_index].set(token_grad)]
  transfers between devices with their start and end apart: 4 -> 0, of which waited for: 3 -> 0; matrix products, arithmetic and copies ran while one was open for 9% -> 0% of each run, Pallas kernels for 0% -> 0%
where the time goes in v1:
time: 139 us
  Pallas kernels  129 us (93%)
  local copies, waits for them, and re-layouts  9.35 us (7%)
    pallas_call x1, Pallas kernels, per_device(): pl.pallas_call(functools.partial(kernel, z_n, z_lo, cores, xy_n, cap), ou...  129 us
    unnamed x2, local copies, waits for them, and re-layouts  9.35 us

profile of v1, /device:TPU:1, one launch (start us, length us, event | category | flops | bytes accessed | tf_op | source)
XLA Modules:
  0.0 138.7 jit_solution(933053652664576828)
XLA Ops:
  0.0 1.5 %copy.4.owner_ref = s32[256,1]{1,0:T(8,128)} copy(s32[256,1]{0,1:T(1,128)} %param.4) | data formatting | bytes 2048 | tf_op args[1]
  1.5 129.4 %shard_map.37 = bf16[1000,4608]{1,0:T(8,128)(2,1)} custom-call(bf16[256,4608]{1,0:T(8,128)(2,1)} %x_ref.1, s32[256,1]{1,0:T(8,128)} %copy.4.owner_ref, s32[1,256]{1,0:T(1,128)} %bitcast.1), custom_call_target="tpu_custom_call" | custom-call | tf_op jit(solution)/shard_map/pallas_call | solution.py:209
  130.9 7.9 %copy.6 = bf16[1000,4608]{1,0:T(8,128)(2,1)} copy(bf16[1000,4608]{1,0:T(8,128)(2,1)} %shard_map.37) | data formatting | bytes 18432000
